TPU v7x, 512 devices: a whole 4x4x16 slice. The times are simulated.
512 devices in a mesh: dom: 128 (over y, z, core), field: 4 (over x).
Axes of the slice: x: 4, y: 4, z: 16, core: 2. Of those that a mesh axis runs over, the one named last changes fastest.
Arguments:
- adjoint: bfloat16 [1024, 384, 128], P('dom', 'field'), may hold values from -6 to 6
- face_blocks: bfloat16 [4480, 384, 384], P('dom', 'field'), may hold values from -0.3125 to 0.3125
- diag_blocks: bfloat16 [1024, 384, 384], P('dom', 'field'), may hold values from -0.3125 to 0.3125
- face_left: int32 [4480], P('dom'), may hold values from 0 to 7
- face_right: int32 [4480], P('dom'), may hold values from 0 to 7
- face_code: int32 [4480], P('dom'), may hold values from 0 to 7
- side_counts: int32 [128, 5], P('dom'), may hold values from 1 to 7, 24 in all within a row
Outputs:
- psi: bfloat16 [1024, 384, 128], P('dom', 'field')
- second: bfloat16 [1024, 384, 128], P('dom', 'field')
Inputs may be any that keep to these rules, and one draw needn't show every extreme that they name: `side_counts`: the 5 lists of one partition hold 24 live faces together, each list at least one, and some list of every partition is full with 7. `face_right`: slots at or beyond a list's count are unused; their indices and blocks are arbitrary.
All inputs are finite; a program needn't handle non-finite values.
Results may differ from a plain program's by a relative error of at most 0.0049.
Values may be sent and summed in bfloat16 or wider, within the bound.
No kernel may reach another device: no remote copies, remote signals or barrier semaphores. Data moves between devices by JAX's collectives and lax.ppermute only.
A program may use at most 64 MiB of HBM per device.

v0:
```python
import jax
import jax.numpy as jnp
from jax import lax
from jax.sharding import PartitionSpec as P

PTS = 4
NS = 5


def from_behind(array, axis, by):
    peers = lax.axis_size(axis)
    return lax.ppermute(array, axis, [(i, (i + by) % peers) for i in range(peers)])


def orient(blocks, orient_code):
    number = blocks.shape[0]
    shaped = blocks.reshape(number, blocks.shape[1] // (PTS * PTS), PTS, PTS, blocks.shape[2])
    flip_rows = (orient_code % 2 == 1)[:, None, None, None, None]
    flip_cols = (orient_code // 2 % 2 == 1)[:, None, None, None, None]
    swap_both = (orient_code >= 4)[:, None, None, None, None]
    shaped = jnp.where(flip_rows, jnp.flip(shaped, 2), shaped)
    shaped = jnp.where(flip_cols, jnp.flip(shaped, 3), shaped)
    shaped = jnp.where(swap_both, jnp.swapaxes(shaped, 2, 3), shaped)
    return shaped.reshape(blocks.shape)


def deposit(summed, product, targets):
    n_elems = summed.shape[0]
    onehot = (targets[None, :] == jnp.arange(n_elems, dtype=jnp.int32)[:, None]).astype(jnp.float32)
    return summed + jnp.einsum("ec,cxk->exk", onehot, product, precision=lax.Precision.HIGHEST)


def local(adjoint, face_blocks, diag_blocks, face_left, face_right, face_code, side_counts):
    n_domains = lax.axis_size("dom")
    stride = n_domains // 8
    offsets = [0, 1, -1, stride, -stride]
    capacity = face_blocks.shape[0] // NS
    slot_index = jnp.arange(capacity, dtype=jnp.int32)
    live_flags = (slot_index[None, :] < side_counts[0][:, None]).reshape(NS * capacity)
    oriented = orient(face_blocks, face_code)
    prepared = jnp.where(live_flags[:, None, None], oriented, jnp.zeros_like(oriented))
    targets = face_right.reshape(NS, capacity)
    sources = face_left.reshape(NS, capacity)
    target_list = [targets[0]]
    for side in range(1, NS):
        target_list.append(from_behind(targets[side], "dom", offsets[side]))
    all_targets = jnp.concatenate(target_list, 0)
    block_sides = prepared.reshape(NS, capacity, prepared.shape[1], prepared.shape[2])
    moved = [block_sides[0]]
    for side in range(1, NS):
        moved.append(from_behind(block_sides[side], "dom", offsets[side]))
    all_blocks = jnp.concatenate(moved, 0)

    def apply_op(vector):
        whole = lax.all_gather(vector, "field", axis=1, tiled=True)
        summed = jnp.einsum("ecr,erk->eck", diag_blocks, whole, preferred_element_type=jnp.float32)
        row_list = [jnp.take(whole, sources[0], axis=0)]
        for side in range(1, NS):
            halo_rows = jnp.take(vector, sources[side], axis=0)
            landed = from_behind(halo_rows, "dom", offsets[side])
            row_list.append(lax.all_gather(landed, "field", axis=1, tiled=True))
        rows_all = jnp.concatenate(row_list, 0)
        product = jnp.einsum(
            "scr,srk->sck", all_blocks, rows_all, preferred_element_type=jnp.float32
        )
        return deposit(summed, product, all_targets)

    first = apply_op(adjoint)
    psi = (adjoint.astype(jnp.float32) - 0.5 * first).astype(jnp.bfloat16)
    second = apply_op(psi).astype(jnp.bfloat16)
    return (psi, second)


def solution(mesh):
    return jax.shard_map(
        local,
        mesh=mesh,
        in_specs=(
            P("dom", "field", None),
            P("dom", "field", None),
            P("dom", "field", None),
            P("dom"),
            P("dom"),
            P("dom"),
            P("dom", None),
        ),
        out_specs=(P("dom", "field", None), P("dom", "field", None)),
        check_vma=False,
    )
```

profile of v0, /device:TPU:466, one launch (start us, length us, event | category | flops | bytes accessed | tf_op | source)
XLA Modules:
  0.0 374.7 jit_solution(1725992629330623298)
XLA Ops:
  0.7 4.4 %reshape.72 = bf16[35,6,4,4,384]{4,3,2,1,0:T(4,128)(2,1)S(1)} reshape(bf16[35,96,384]{2,1,0:T(8,128)(2,1)} %param.12) | data formatting | bytes 5160960 | tf_op jit(solution)/shard_map/reshape | solution.py:17
  5.1 3.2 reverse_select_fusion
  8.3 15.0 %rev.9 = bf16[35,6,4,4,384]{4,3,2,1,0:T(4,128)(2,1)} reverse(bf16[35,6,4,4,384]{4,3,2,1,0:T(4,128)(2,1)} %reverse_select_fusion), dimensions={3} | reverse | bytes 5160960 | tf_op jit(solution)/shard_map/jit(_flip)/rev | solution.py:22
  23.3 5.2 %broadcast_select_fusion = bf16[35,6,4,4,384]{4,3,2,1,0:T(4,128)(2,1)S(1)} fusion(bf16[35,6,4,4,384]{4,3,2,1,0:T(4,128)(2,1)} %rev.9, pred[35]{0:T(512)(128)(4,1)S(1)} %get-tuple-element.34, bf16[35,6,4,4,384]{4,3,2,1,0:T(4,128)(2,1)S(1)} %reshape.72, pred[35]{0:T(512)(128)(4,1)S(1)} %get-tuple-element.33), kind=kLoop, calls=%fused_computation.12 | loop fusion | flops 2580480 | bytes 7741510 | tf_op jit(solution)/shard_map/jit(_where)/select_n | solution.py:22
  28.5 3.1 bitcast_select_fusion
  31.5 4.1 %reshape.73 = bf16[35,96,384]{2,1,0:T(8,128)(2,1)S(1)} reshape(bf16[35,6,4,4,384]{4,3,2,1,0:T(4,128)(2,1)} %bitcast_select_fusion) | data formatting | bytes 5160960 | tf_op jit(solution)/shard_map/reshape | solution.py:24
  36.2 1.5 fusion.17
  37.6 1.9 collective-permute-start.4
  39.6 3.6 collective-permute-start.5
  43.2 6.2 %collective-permute-start.6 = (bf16[7,96,384]{2,1,0:T(8,128)(2,1)}, bf16[7,96,384]{2,1,0:T(8,128)(2,1)}, u32[]{:S(2)}, u32[]{:S(2)}) collective-permute-start(bf16[7,96,384]{2,1,0:T(8,128)(2,1)} %get-tuple-element.15), channel_id=1, source_target_pairs={{0,64},{4,68},{8,72},{12,76},{16,80},{20,84},{24,88},{28,92},{32,9... | collective-permute-start | bytes 1548296 | tf_op jit(solution)/shard_map/ppermute | solution.py:12
  51.4 1.9 collective-permute-start.8
  54.0 3.9 %collective-permute-start = (s32[7]{0:T(128)}, s32[7]{0:T(128)}, u32[]{:S(2)}, u32[]{:S(2)}) collective-permute-start(s32[7]{0:T(128)} %get-tuple-element.21), channel_id=1, source_target_pairs={{0,4},{4,8},{8,12},{12,16},{16,20},{20,24},{24,28},{28,32},{32,36}... | collective-permute-start | bytes 92 | tf_op jit(solution)/shard_map/ppermute | solution.py:12
  57.9 15.1 %all_gather.30 = bf16[8,384,128]{2,1,0:T(8,128)(2,1)} all-gather(bf16[8,96,128]{2,1,0:T(8,128)(2,1)S(1)} %copy-done.3), channel_id=1, replica_groups=mesh['dom'=128,'field'=4] {'field'}, dimensions={1}, use_global_device_ids=true | all-gather | bytes 983040 | tf_op jit(solution)/shard_map/all_gather | solution.py:55
  75.0 1.2 gather_fusion.3
  76.2 1.3 pad_clamp_fusion
  77.5 1.4 gather_fusion.4
  78.8 2.6 gather_fusion
  81.5 2.2 select_dynamic-update-slice_fusion.1
  83.6 1.4 broadcast_select_fusion.7
  85.0 1.7 broadcast_select_fusion.5
  86.7 1.0 broadcast_select_fusion.3
  87.7 3.0 collective-permute-done
  90.7 1.9 collective-permute-start.1
  92.6 5.7 %collective-permute-done.1 = s32[7]{0:T(128)} collective-permute-done((s32[7]{0:T(128)}, s32[7]{0:T(128)}, u32[]{:S(2)}, u32[]{:S(2)}) %collective-permute-start.1) | collective-permute-done | bytes 60 | tf_op jit(solution)/shard_map/ppermute | solution.py:12
  98.3 8.8 %collective-permute-start.2 = (s32[7]{0:T(128)}, s32[7]{0:T(128)}, u32[]{:S(2)}, u32[]{:S(2)}) collective-permute-start(s32[7]{0:T(128)} %get-tuple-element.23), channel_id=1, source_target_pairs={{0,64},{4,68},{8,72},{12,76},{16,80},{20,84},{24,88},{28,92},{32,9... | collective-permute-start | bytes 92 | tf_op jit(solution)/shard_map/ppermute | solution.py:12
  107.1 5.4 %collective-permute-done.2 = s32[7]{0:T(128)} collective-permute-done((s32[7]{0:T(128)}, s32[7]{0:T(128)}, u32[]{:S(2)}, u32[]{:S(2)}) %collective-permute-start.2) | collective-permute-done | bytes 60 | tf_op jit(solution)/shard_map/ppermute | solution.py:12
  112.5 9.0 %collective-permute-start.3 = (s32[7]{0:T(128)}, s32[7]{0:T(128)}, u32[]{:S(2)}, u32[]{:S(2)}) collective-permute-start(s32[7]{0:T(128)} %get-tuple-element.19), channel_id=1, source_target_pairs={{0,448},{4,452},{8,456},{12,460},{16,464},{20,468},{24,472},{28,47... | collective-permute-start | bytes 92 | tf_op jit(solution)/shard_map/ppermute | solution.py:12
  121.5 6.2 %collective-permute-done.3 = s32[7]{0:T(128)} collective-permute-done((s32[7]{0:T(128)}, s32[7]{0:T(128)}, u32[]{:S(2)}, u32[]{:S(2)}) %collective-permute-start.3) | collective-permute-done | bytes 60 | tf_op jit(solution)/shard_map/ppermute | solution.py:12
  127.7 8.1 %collective-permute-start.7 = (bf16[7,96,384]{2,1,0:T(8,128)(2,1)}, bf16[7,96,384]{2,1,0:T(8,128)(2,1)}, u32[]{:S(2)}, u32[]{:S(2)}) collective-permute-start(bf16[7,96,384]{2,1,0:T(8,128)(2,1)} %get-tuple-element.14), channel_id=1, source_target_pairs={{0,448},{4,452},{8,456},{12,460},{16,464},{20,468},{24,472},{28,47... | collective-permute-start | bytes 1548296 | tf_op jit(solution)/shard_map/ppermute | solution.py:12
  135.8 1.4 concatenate.12
  137.2 1.9 collective-permute-start.9
  139.1 14.2 %all_gather.31 = bf16[7,384,128]{2,1,0:T(8,128)(2,1)S(1)} all-gather(bf16[7,96,128]{2,1,0:T(8,128)(2,1)} %collective-permute-done.8), channel_id=1, replica_groups=mesh['dom'=128,'field'=4] {'field'}, dimensions={1}, use_global_device_ids=true | all-gather | bytes 860160 | tf_op jit(solution)/shard_map/all_gather | solution.py:61
  153.3 35.4 %collective-permute-done.9 = bf16[7,96,128]{2,1,0:T(8,128)(2,1)S(1)} collective-permute-done((bf16[7,96,128]{2,1,0:T(8,128)(2,1)}, bf16[7,96,128]{2,1,0:T(8,128)(2,1)S(1)}, u32[]{:S(2)}, u32[]{:S(2)}) %collective-permute-start.9) | collective-permute-done | bytes 172064 | tf_op jit(solution)/shard_map/ppermute | solution.py:12
  188.7 1.9 collective-permute-start.10
  190.7 14.3 %all_gather.32 = bf16[7,384,128]{2,1,0:T(8,128)(2,1)S(1)} all-gather(bf16[7,96,128]{2,1,0:T(8,128)(2,1)S(1)} %collective-permute-done.9), channel_id=1, replica_groups=mesh['dom'=128,'field'=4] {'field'}, dimensions={1}, use_global_device_ids=true | all-gather | bytes 860160 | tf_op jit(solution)/shard_map/all_gather | solution.py:61
  204.9 3.1 collective-permute-done.10
  208.0 9.5 %collective-permute-start.11 = (bf16[7,96,128]{2,1,0:T(8,128)(2,1)S(1)}, bf16[7,96,128]{2,1,0:T(8,128)(2,1)S(1)}, u32[]{:S(2)}, u32[]{:S(2)}) collective-permute-start(bf16[7,96,128]{2,1,0:T(8,128)(2,1)S(1)} %broadcast_select_fusion.3), channel_id=1, source_target_pairs={{0,448},{4,452},{8,456},{12,460},{16,464},{20,468},{24,472},{28,47... | collective-permute-start | bytes 516104 | tf_op jit(solution)/shard_map/ppermute | solution.py:12
  217.5 13.1 %all_gather.33 = bf16[7,384,128]{2,1,0:T(8,128)(2,1)S(1)} all-gather(bf16[7,96,128]{2,1,0:T(8,128)(2,1)S(1)} %collective-permute-done.10), channel_id=1, replica_groups=mesh['dom'=128,'field'=4] {'field'}, dimensions={1}, use_global_device_ids=true | all-gather | bytes 860160 | tf_op jit(solution)/shard_map/all_gather | solution.py:61
  230.6 13.9 %all_gather.34 = bf16[7,384,128]{2,1,0:T(8,128)(2,1)S(1)} all-gather(bf16[7,96,128]{2,1,0:T(8,128)(2,1)S(1)} %collective-permute-done.11), channel_id=1, replica_groups=mesh['dom'=128,'field'=4] {'field'}, dimensions={1}, use_global_device_ids=true | all-gather | bytes 860160 | tf_op jit(solution)/shard_map/all_gather | solution.py:61
  248.1 1.3 constant_dynamic-update-slice_fusion.3
  249.4 1.1 constant_dynamic-update-slice_fusion.2
  250.5 1.1 constant_dynamic-update-slice_fusion.1
  251.7 1.1 constant_dynamic-update-slice_fusion
  253.7 1.7 fusion.2
  256.5 14.0 %all_gather.35 = bf16[8,384,128]{2,1,0:T(8,128)(2,1)} all-gather(bf16[8,96,128]{2,1,0:T(8,128)(2,1)S(1)} %fusion.7), channel_id=1, replica_groups=mesh['dom'=128,'field'=4] {'field'}, dimensions={1}, use_global_device_ids=true | all-gather | bytes 983040 | tf_op jit(solution)/shard_map/all_gather | solution.py:55
  270.6 2.2 gather_fusion.6
  272.7 2.2 gather_fusion.7
  274.9 1.5 gather_fusion.8
  276.4 1.6 gather_fusion.9
  278.1 2.7 gather_fusion.5
  280.7 1.0 broadcast_select_fusion.8
  281.7 1.9 collective-permute-start.12
  283.7 1.0 broadcast_select_fusion.6
  284.7 3.6 collective-permute-start.13
  288.4 6.2 %collective-permute-start.14 = (bf16[7,96,128]{2,1,0:T(8,128)(2,1)S(1)}, bf16[7,96,128]{2,1,0:T(8,128)(2,1)S(1)}, u32[]{:S(2)}, u32[]{:S(2)}) collective-permute-start(bf16[7,96,128]{2,1,0:T(8,128)(2,1)S(1)} %broadcast_select_fusion.4), channel_id=1, source_target_pairs={{0,64},{4,68},{8,72},{12,76},{16,80},{20,84},{24,88},{28,92},{32,9... | collective-permute-start | bytes 516104 | tf_op jit(solution)/shard_map/ppermute | solution.py:12
  294.8 8.3 %collective-permute-start.15 = (bf16[7,96,128]{2,1,0:T(8,128)(2,1)S(1)}, bf16[7,96,128]{2,1,0:T(8,128)(2,1)S(1)}, u32[]{:S(2)}, u32[]{:S(2)}) collective-permute-start(bf16[7,96,128]{2,1,0:T(8,128)(2,1)S(1)} %broadcast_select_fusion.2), channel_id=1, source_target_pairs={{0,448},{4,452},{8,456},{12,460},{16,464},{20,468},{24,472},{28,47... | collective-permute-start | bytes 516104 | tf_op jit(solution)/shard_map/ppermute | solution.py:12
  303.1 1.3 select_dynamic-update-slice_fusion
  304.4 12.6 %collective-permute-done.12 = bf16[7,96,128]{2,1,0:T(8,128)(2,1)S(1)} collective-permute-done((bf16[7,96,128]{2,1,0:T(8,128)(2,1)S(1)}, bf16[7,96,128]{2,1,0:T(8,128)(2,1)S(1)}, u32[]{:S(2)}, u32[]{:S(2)}) %collective-permute-start.12) | collective-permute-done | bytes 172064 | tf_op jit(solution)/shard_map/ppermute | solution.py:12
  317.1 13.1 %all_gather.36 = bf16[7,384,128]{2,1,0:T(8,128)(2,1)S(1)} all-gather(bf16[7,96,128]{2,1,0:T(8,128)(2,1)S(1)} %collective-permute-done.12), channel_id=1, replica_groups=mesh['dom'=128,'field'=4] {'field'}, dimensions={1}, use_global_device_ids=true | all-gather | bytes 860160 | tf_op jit(solution)/shard_map/all_gather | solution.py:61
  330.2 14.2 %all_gather.37 = bf16[7,384,128]{2,1,0:T(8,128)(2,1)S(1)} all-gather(bf16[7,96,128]{2,1,0:T(8,128)(2,1)S(1)} %collective-permute-done.13), channel_id=1, replica_groups=mesh['dom'=128,'field'=4] {'field'}, dimensions={1}, use_global_device_ids=true | all-gather | bytes 860160 | tf_op jit(solution)/shard_map/all_gather | solution.py:61
  344.5 13.1 %all_gather.38 = bf16[7,384,128]{2,1,0:T(8,128)(2,1)S(1)} all-gather(bf16[7,96,128]{2,1,0:T(8,128)(2,1)S(1)} %collective-permute-done.14), channel_id=1, replica_groups=mesh['dom'=128,'field'=4] {'field'}, dimensions={1}, use_global_device_ids=true | all-gather | bytes 860160 | tf_op jit(solution)/shard_map/all_gather | solution.py:61
  357.8 13.1 %all_gather.39 = bf16[7,384,128]{2,1,0:T(8,128)(2,1)S(1)} all-gather(bf16[7,96,128]{2,1,0:T(8,128)(2,1)S(1)} %collective-permute-done.15), channel_id=1, replica_groups=mesh['dom'=128,'field'=4] {'field'}, dimensions={1}, use_global_device_ids=true | all-gather | bytes 860160 | tf_op jit(solution)/shard_map/all_gather | solution.py:61
  371.9 1.7 fusion
  373.6 1.0 fusion.8
  (69 shorter events, 12.1 us)
Async XLA Ops:
  0.6 254.8 %copy-start = (bf16[8,96,384]{2,1,0:T(8,128)(2,1)S(1)}, bf16[8,96,384]{2,1,0:T(8,128)(2,1)}, u32[]{:S(2)}) copy-start(bf16[8,96,384]{2,1,0:T(8,128)(2,1)} %param.13) | copy-start | bytes 1769476
  0.6 4.4 %copy-start.15 = (s32[35]{0:T(128)S(1)}, s32[35]{0:T(128)}, u32[]{:S(2)}) copy-start(s32[35]{0:T(128)} %param.16) | copy-start | bytes 424
  31.5 4.1 %copy-start.16 = (s32[1,5]{1,0:T(1,128)S(1)}, s32[1,5]{1,0:T(1,128)}, u32[]{:S(2)}) copy-start(s32[1,5]{1,0:T(1,128)} %param.17) | copy-start | bytes 64
  36.1 13.2 %copy-start.7 = (s32[35]{0:T(128)S(1)}, s32[35]{0:T(128)}, u32[]{:S(2)}) copy-start(s32[35]{0:T(128)} %param.14) | copy-start | bytes 424
  36.2 13.9 %copy-start.3 = (bf16[8,96,128]{2,1,0:T(8,128)(2,1)S(1)}, bf16[8,96,128]{2,1,0:T(8,128)(2,1)}, u32[]{:S(2)}) copy-start(bf16[8,96,128]{2,1,0:T(8,128)(2,1)} %param.11) | copy-start | bytes 589828
  36.2 17.2 %copy-start.6 = (s32[35]{0:T(128)S(1)}, s32[35]{0:T(128)}, u32[]{:S(2)}) copy-start(s32[35]{0:T(128)} %param.15) | copy-start | bytes 424
  37.6 210.5 %collective-permute-start.4 = (bf16[7,96,384]{2,1,0:T(8,128)(2,1)}, bf16[7,96,384]{2,1,0:T(8,128)(2,1)}, u32[]{:S(2)}, u32[]{:S(2)}) collective-permute-start(bf16[7,96,384]{2,1,0:T(8,128)(2,1)} %get-tuple-element.17), channel_id=1, source_target_pairs={{0,4},{4,8},{8,12},{12,16},{16,20},{20,24},{24,28},{28,32},{32,36}... | collective-permute-start | bytes 1548296 | tf_op jit(solution)/shard_map/ppermute | solution.py:12
  39.6 209.8 %collective-permute-start.5 = (bf16[7,96,384]{2,1,0:T(8,128)(2,1)}, bf16[7,96,384]{2,1,0:T(8,128)(2,1)}, u32[]{:S(2)}, u32[]{:S(2)}) collective-permute-start(bf16[7,96,384]{2,1,0:T(8,128)(2,1)} %get-tuple-element.16), channel_id=1, source_target_pairs={{0,508},{4,0},{8,4},{12,8},{16,12},{20,16},{24,20},{28,24},{32,28}... | collective-permute-start | bytes 1548296 | tf_op jit(solution)/shard_map/ppermute | solution.py:12
  43.2 207.3 %collective-permute-start.6 = (bf16[7,96,384]{2,1,0:T(8,128)(2,1)}, bf16[7,96,384]{2,1,0:T(8,128)(2,1)}, u32[]{:S(2)}, u32[]{:S(2)}) collective-permute-start(bf16[7,96,384]{2,1,0:T(8,128)(2,1)} %get-tuple-element.15), channel_id=1, source_target_pairs={{0,64},{4,68},{8,72},{12,76},{16,80},{20,84},{24,88},{28,92},{32,9... | collective-permute-start | bytes 1548296 | tf_op jit(solution)/shard_map/ppermute | solution.py:12
  50.0 23.7 %copy-start.13 = (pred[7]{0:T(512)(128)(4,1)}, pred[7]{0:T(512)(128)(4,1)S(1)}, u32[]{:S(2)}) copy-start(pred[7]{0:T(512)(128)(4,1)S(1)} %get-tuple-element.26) | copy-start | bytes 25
  51.4 85.8 %collective-permute-start.8 = (bf16[7,96,128]{2,1,0:T(8,128)(2,1)}, bf16[7,96,128]{2,1,0:T(8,128)(2,1)}, u32[]{:S(2)}, u32[]{:S(2)}) collective-permute-start(bf16[7,96,128]{2,1,0:T(8,128)(2,1)} %broadcast_select_fusion.9), channel_id=1, source_target_pairs={{0,4},{4,8},{8,12},{12,16},{16,20},{20,24},{24,28},{28,32},{32,36}... | collective-permute-start | bytes 516104 | tf_op jit(solution)/shard_map/ppermute | solution.py:12
  54.0 36.7 %collective-permute-start = (s32[7]{0:T(128)}, s32[7]{0:T(128)}, u32[]{:S(2)}, u32[]{:S(2)}) collective-permute-start(s32[7]{0:T(128)} %get-tuple-element.21), channel_id=1, source_target_pairs={{0,4},{4,8},{8,12},{12,16},{16,20},{20,24},{24,28},{28,32},{32,36}... | collective-permute-start | bytes 92 | tf_op jit(solution)/shard_map/ppermute | solution.py:12
  90.7 7.6 %collective-permute-start.1 = (s32[7]{0:T(128)}, s32[7]{0:T(128)}, u32[]{:S(2)}, u32[]{:S(2)}) collective-permute-start(s32[7]{0:T(128)} %get-tuple-element.20), channel_id=1, source_target_pairs={{0,508},{4,0},{8,4},{12,8},{16,12},{20,16},{24,20},{28,24},{32,28}... | collective-permute-start | bytes 92 | tf_op jit(solution)/shard_map/ppermute | solution.py:12
  98.3 14.2 %collective-permute-start.2 = (s32[7]{0:T(128)}, s32[7]{0:T(128)}, u32[]{:S(2)}, u32[]{:S(2)}) collective-permute-start(s32[7]{0:T(128)} %get-tuple-element.23), channel_id=1, source_target_pairs={{0,64},{4,68},{8,72},{12,76},{16,80},{20,84},{24,88},{28,92},{32,9... | collective-permute-start | bytes 92 | tf_op jit(solution)/shard_map/ppermute | solution.py:12
  112.5 15.2 %collective-permute-start.3 = (s32[7]{0:T(128)}, s32[7]{0:T(128)}, u32[]{:S(2)}, u32[]{:S(2)}) collective-permute-start(s32[7]{0:T(128)} %get-tuple-element.19), channel_id=1, source_target_pairs={{0,448},{4,452},{8,456},{12,460},{16,464},{20,468},{24,472},{28,47... | collective-permute-start | bytes 92 | tf_op jit(solution)/shard_map/ppermute | solution.py:12
  127.7 124.0 %collective-permute-start.7 = (bf16[7,96,384]{2,1,0:T(8,128)(2,1)}, bf16[7,96,384]{2,1,0:T(8,128)(2,1)}, u32[]{:S(2)}, u32[]{:S(2)}) collective-permute-start(bf16[7,96,384]{2,1,0:T(8,128)(2,1)} %get-tuple-element.14), channel_id=1, source_target_pairs={{0,448},{4,452},{8,456},{12,460},{16,464},{20,468},{24,472},{28,47... | collective-permute-start | bytes 1548296 | tf_op jit(solution)/shard_map/ppermute | solution.py:12
  137.2 51.5 %collective-permute-start.9 = (bf16[7,96,128]{2,1,0:T(8,128)(2,1)}, bf16[7,96,128]{2,1,0:T(8,128)(2,1)S(1)}, u32[]{:S(2)}, u32[]{:S(2)}) collective-permute-start(bf16[7,96,128]{2,1,0:T(8,128)(2,1)} %broadcast_select_fusion.7), channel_id=1, source_target_pairs={{0,508},{4,0},{8,4},{12,8},{16,12},{20,16},{24,20},{28,24},{32,28}... | collective-permute-start | bytes 516104 | tf_op jit(solution)/shard_map/ppermute | solution.py:12
  188.7 19.2 %collective-permute-start.10 = (bf16[7,96,128]{2,1,0:T(8,128)(2,1)}, bf16[7,96,128]{2,1,0:T(8,128)(2,1)S(1)}, u32[]{:S(2)}, u32[]{:S(2)}) collective-permute-start(bf16[7,96,128]{2,1,0:T(8,128)(2,1)} %broadcast_select_fusion.5), channel_id=1, source_target_pairs={{0,64},{4,68},{8,72},{12,76},{16,80},{20,84},{24,88},{28,92},{32,9... | collective-permute-start | bytes 516104 | tf_op jit(solution)/shard_map/ppermute | solution.py:12
  208.0 22.7 %collective-permute-start.11 = (bf16[7,96,128]{2,1,0:T(8,128)(2,1)S(1)}, bf16[7,96,128]{2,1,0:T(8,128)(2,1)S(1)}, u32[]{:S(2)}, u32[]{:S(2)}) collective-permute-start(bf16[7,96,128]{2,1,0:T(8,128)(2,1)S(1)} %broadcast_select_fusion.3), channel_id=1, source_target_pairs={{0,448},{4,452},{8,456},{12,460},{16,464},{20,468},{24,472},{28,47... | collective-permute-start | bytes 516104 | tf_op jit(solution)/shard_map/ppermute | solution.py:12
  248.1 4.7 %copy-start.5 = (bf16[35,384,128]{2,1,0:T(8,128)(2,1)S(1)}, bf16[35,384,128]{2,1,0:T(8,128)(2,1)}, u32[]{:S(2)}) copy-start(bf16[35,384,128]{2,1,0:T(8,128)(2,1)} %constant_dynamic-update-slice_fusion.4) | copy-start | bytes 10321924
  252.8 0.9 copy-start.9
  253.7 1.7 copy-start.1
  255.5 25.3 %copy-start.14 = (pred[7]{0:T(512)(128)(4,1)S(1)}, pred[7]{0:T(512)(128)(4,1)}, u32[]{:S(2)}) copy-start(pred[7]{0:T(512)(128)(4,1)} %copy-done.13) | copy-start | bytes 25
  255.8 0.7 copy-start.4
  256.5 27.2 %copy-start.12 = (pred[7]{0:T(512)(128)(4,1)S(1)}, pred[7]{0:T(512)(128)(4,1)}, u32[]{:S(2)}) copy-start(pred[7]{0:T(512)(128)(4,1)} %get-tuple-element.24) | copy-start | bytes 25
  256.5 31.8 %copy-start.11 = (pred[7]{0:T(512)(128)(4,1)S(1)}, pred[7]{0:T(512)(128)(4,1)}, u32[]{:S(2)}) copy-start(pred[7]{0:T(512)(128)(4,1)} %get-tuple-element.30) | copy-start | bytes 25
  256.5 38.2 %copy-start.10 = (pred[7]{0:T(512)(128)(4,1)S(1)}, pred[7]{0:T(512)(128)(4,1)}, u32[]{:S(2)}) copy-start(pred[7]{0:T(512)(128)(4,1)} %get-tuple-element.4) | copy-start | bytes 25
  256.5 46.6 %copy-start.8 = (pred[7]{0:T(512)(128)(4,1)S(1)}, pred[7]{0:T(512)(128)(4,1)}, u32[]{:S(2)}) copy-start(pred[7]{0:T(512)(128)(4,1)} %get-tuple-element.28) | copy-start | bytes 25
  281.7 35.3 %collective-permute-start.12 = (bf16[7,96,128]{2,1,0:T(8,128)(2,1)S(1)}, bf16[7,96,128]{2,1,0:T(8,128)(2,1)S(1)}, u32[]{:S(2)}, u32[]{:S(2)}) collective-permute-start(bf16[7,96,128]{2,1,0:T(8,128)(2,1)S(1)} %broadcast_select_fusion.8), channel_id=1, source_target_pairs={{0,4},{4,8},{8,12},{12,16},{16,20},{20,24},{24,28},{28,32},{32,36}... | collective-permute-start | bytes 516104 | tf_op jit(solution)/shard_map/ppermute | solution.py:12
  284.7 45.5 %collective-permute-start.13 = (bf16[7,96,128]{2,1,0:T(8,128)(2,1)S(1)}, bf16[7,96,128]{2,1,0:T(8,128)(2,1)S(1)}, u32[]{:S(2)}, u32[]{:S(2)}) collective-permute-start(bf16[7,96,128]{2,1,0:T(8,128)(2,1)S(1)} %broadcast_select_fusion.6), channel_id=1, source_target_pairs={{0,508},{4,0},{8,4},{12,8},{16,12},{20,16},{24,20},{28,24},{32,28}... | collective-permute-start | bytes 516104 | tf_op jit(solution)/shard_map/ppermute | solution.py:12
  288.4 56.1 %collective-permute-start.14 = (bf16[7,96,128]{2,1,0:T(8,128)(2,1)S(1)}, bf16[7,96,128]{2,1,0:T(8,128)(2,1)S(1)}, u32[]{:S(2)}, u32[]{:S(2)}) collective-permute-start(bf16[7,96,128]{2,1,0:T(8,128)(2,1)S(1)} %broadcast_select_fusion.4), channel_id=1, source_target_pairs={{0,64},{4,68},{8,72},{12,76},{16,80},{20,84},{24,88},{28,92},{32,9... | collective-permute-start | bytes 516104 | tf_op jit(solution)/shard_map/ppermute | solution.py:12
  294.8 63.0 %collective-permute-start.15 = (bf16[7,96,128]{2,1,0:T(8,128)(2,1)S(1)}, bf16[7,96,128]{2,1,0:T(8,128)(2,1)S(1)}, u32[]{:S(2)}, u32[]{:S(2)}) collective-permute-start(bf16[7,96,128]{2,1,0:T(8,128)(2,1)S(1)} %broadcast_select_fusion.2), channel_id=1, source_target_pairs={{0,448},{4,452},{8,456},{12,460},{16,464},{20,468},{24,472},{28,47... | collective-permute-start | bytes 516104 | tf_op jit(solution)/shard_map/ppermute | solution.py:12
  371.9 1.7 copy-start.2
where the time goes:
time: 377 us; the launch traced here: 375 us
  blocking collectives  138 us (37%)
  starting transfers between devices  78.8 us (21%)
  waiting for transfers between devices  71.4 us (19%)
  local copies, waits for them, and re-layouts  53 us (14%)
  other arithmetic  25.6 us (7%)
  matrix products  6.55 us (2%)
    all_gather x8, blocking collectives, apply_op(): row_list.append(lax.all_gather(landed, 'field', axis=1, tiled=True))  109 us
    ppermute x16, starting transfers between devices, from_behind(): lax.ppermute(array, axis, [(i, (i + by) % peers) for i in range(peers)])  78.8 us
    ppermute x16, waiting for transfers between devices, from_behind(): lax.ppermute(array, axis, [(i, (i + by) % peers) for i in range(peers)])  71.4 us
    all_gather x2, blocking collectives, apply_op(): whole = lax.all_gather(vector, 'field', axis=1, tiled=True)  29.1 us
    rev x1, local copies, waits for them, and re-layouts, orient(): shaped = jnp.where(flip_cols, jnp.flip(shaped, 3), shaped)  15 us
    gather x8, local copies, waits for them, and re-layouts, apply_op(): halo_rows = jnp.take(vector, sources[side], axis=0)  11.2 us
  transfers between devices with their start and end apart: 16, of which 7 were waited for; matrix products, arithmetic and copies ran while one was open for 8% of the time, Pallas kernels for 0%

commit v1 on v0

--- a/solution.py
+++ b/solution.py
@@ -58,7 +58,11 @@
         for side in range(1, NS):
             halo_rows = jnp.take(vector, sources[side], axis=0)
             landed = from_behind(halo_rows, "dom", offsets[side])
-            row_list.append(lax.all_gather(landed, "field", axis=1, tiled=True))
+            row_list.append(
+                jnp.concatenate(
+                    lax.all_to_all(jnp.stack(lax.psum(1, "field") * [landed]), "field", 0, 0), 1
+                )
+            )
         rows_all = jnp.concatenate(row_list, 0)
         product = jnp.einsum(
             "scr,srk->sck", all_blocks, rows_all, preferred_element_type=jnp.float32

time: 377 us -> 423 us (1.12)
  the two profiles are of different devices: /device:TPU:466 before, /device:TPU:24 now
where the time goes in v1:
time: 423 us; the launch traced here: 420 us
  waiting for transfers between devices  145 us (34%)
  starting transfers between devices  117 us (28%)
  local copies, waits for them, and re-layouts  77.8 us (18%)
  blocking collectives  43.1 us (10%)
  other arithmetic  24.5 us (6%)
  matrix products  11.2 us (3%)
    ppermute x16, waiting for transfers between devices, from_behind(): lax.ppermute(array, axis, [(i, (i + by) % peers) for i in range(peers)])  142 us
    ppermute x16, starting transfers between devices, from_behind(): lax.ppermute(array, axis, [(i, (i + by) % peers) for i in range(peers)])  80.7 us
    all_gather x2, blocking collectives, apply_op(): whole = lax.all_gather(vector, 'field', axis=1, tiled=True)  43.1 us
    all_to_all x8, starting transfers between devices, apply_op(): lax.all_to_all(jnp.stack(lax.psum(1, 'field') * [landed]), 'field', 0, 0)  36.2 us
    rev x1, local copies, waits for them, and re-layouts, orient(): shaped = jnp.where(flip_cols, jnp.flip(shaped, 3), shaped)  15.1 us
    reshape x8, local copies, waits for them, and re-layouts, apply_op(): jnp.concatenate(lax.all_to_all(jnp.stack(lax.psum(1, 'field') * [landed])...  14.7 us
    unnamed x55, local copies, waits for them, and re-layouts  11 us
    another operation x8, local copies, waits for them, and re-layouts, apply_op(): jnp.stack(lax.psum(1, 'field') * [landed])  9.57 us
  transfers between devices with their start and end apart: 24, of which 9 were waited for; matrix products, arithmetic and copies ran while one was open for 19% of the time, Pallas kernels for 0%

profile of v1, /device:TPU:24, one launch (start us, length us, event | category | flops | bytes accessed | tf_op | source)
XLA Modules:
  0.0 419.9 jit_solution(5023224799269471578)
XLA Ops:
  0.6 1.4 compare_and_fusion
  2.1 1.5 gather_fusion.1
  3.7 1.9 collective-permute-start.8
  5.7 1.5 gather_fusion.2
  7.9 11.1 %collective-permute-start.9 = (bf16[7,96,128]{2,1,0:T(8,128)(2,1)}, bf16[7,96,128]{2,1,0:T(8,128)(2,1)}, u32[]{:S(2)}, u32[]{:S(2)}) collective-permute-start(bf16[7,96,128]{2,1,0:T(8,128)(2,1)} %broadcast_select_fusion.7), channel_id=1, source_target_pairs={{0,508},{4,0},{8,4},{12,8},{16,12},{20,16},{24,20},{28,24},{32,28}... | collective-permute-start | bytes 516104 | tf_op jit(solution)/shard_map/ppermute | solution.py:12
  19.1 4.3 %reshape.136 = bf16[35,6,4,4,384]{4,3,2,1,0:T(4,128)(2,1)S(1)} reshape(bf16[35,96,384]{2,1,0:T(8,128)(2,1)} %param.12) | data formatting | bytes 5160960 | tf_op jit(solution)/shard_map/reshape | solution.py:17
  23.4 3.2 reverse_select_fusion
  26.6 15.1 %rev.9 = bf16[35,6,4,4,384]{4,3,2,1,0:T(4,128)(2,1)} reverse(bf16[35,6,4,4,384]{4,3,2,1,0:T(4,128)(2,1)} %reverse_select_fusion), dimensions={3} | reverse | bytes 5160960 | tf_op jit(solution)/shard_map/jit(_flip)/rev | solution.py:22
  41.7 5.2 %broadcast_select_fusion = bf16[35,6,4,4,384]{4,3,2,1,0:T(4,128)(2,1)S(1)} fusion(bf16[35,6,4,4,384]{4,3,2,1,0:T(4,128)(2,1)} %rev.9, pred[35]{0:T(512)(128)(4,1)S(1)} %get-tuple-element.34, bf16[35,6,4,4,384]{4,3,2,1,0:T(4,128)(2,1)S(1)} %reshape.136, pred[35]{0:T(512)(128)(4,1)S(1)} %get-tuple-element.33), kind=kLoop, calls=%fused_computation.12 | loop fusion | flops 2580480 | bytes 7741510 | tf_op jit(solution)/shard_map/jit(_where)/select_n | solution.py:22
  46.9 3.1 bitcast_select_fusion
  50.0 4.1 reshape.137
  55.2 4.3 %all-to-all-start = ((bf16[4,7,96,128]{3,2,1,0:T(8,128)(2,1)}), bf16[4,7,96,128]{3,2,1,0:T(8,128)(2,1)}, u32[]{:S(2)}, u32[]{:S(2)}) async-start(bf16[4,7,96,128]{3,2,1,0:T(8,128)(2,1)} %stack.16), calls=%async_computation | async-start | bytes 1376256 | tf_op jit(solution)/shard_map/all_to_all | solution.py:63
  59.8 1.4 fusion.17
  61.3 1.9 collective-permute-start.4
  63.2 5.8 %collective-permute-start.5 = (bf16[7,96,384]{2,1,0:T(8,128)(2,1)}, bf16[7,96,384]{2,1,0:T(8,128)(2,1)}, u32[]{:S(2)}, u32[]{:S(2)}) collective-permute-start(bf16[7,96,384]{2,1,0:T(8,128)(2,1)} %get-tuple-element.16), channel_id=1, source_target_pairs={{0,508},{4,0},{8,4},{12,8},{16,12},{20,16},{24,20},{28,24},{32,28}... | collective-permute-start | bytes 1548296 | tf_op jit(solution)/shard_map/ppermute | solution.py:12
  68.9 8.7 %collective-permute-start.6 = (bf16[7,96,384]{2,1,0:T(8,128)(2,1)}, bf16[7,96,384]{2,1,0:T(8,128)(2,1)}, u32[]{:S(2)}, u32[]{:S(2)}) collective-permute-start(bf16[7,96,384]{2,1,0:T(8,128)(2,1)} %get-tuple-element.15), channel_id=1, source_target_pairs={{0,64},{4,68},{8,72},{12,76},{16,80},{20,84},{24,88},{28,92},{32,9... | collective-permute-start | bytes 1548296 | tf_op jit(solution)/shard_map/ppermute | solution.py:12
  77.6 6.8 %collective-permute-start.7 = (bf16[7,96,384]{2,1,0:T(8,128)(2,1)}, bf16[7,96,384]{2,1,0:T(8,128)(2,1)}, u32[]{:S(2)}, u32[]{:S(2)}) collective-permute-start(bf16[7,96,384]{2,1,0:T(8,128)(2,1)} %get-tuple-element.14), channel_id=1, source_target_pairs={{0,448},{4,452},{8,456},{12,460},{16,464},{20,468},{24,472},{28,47... | collective-permute-start | bytes 1548296 | tf_op jit(solution)/shard_map/ppermute | solution.py:12
  85.0 1.9 stack.17
  86.9 4.9 %all-to-all-start.1 = ((bf16[4,7,96,128]{3,2,1,0:T(8,128)(2,1)}), bf16[4,7,96,128]{3,2,1,0:T(8,128)(2,1)}, u32[]{:S(2)}, u32[]{:S(2)}) async-start(bf16[4,7,96,128]{3,2,1,0:T(8,128)(2,1)} %stack.17), calls=%async_computation.1 | async-start | bytes 1376256 | tf_op jit(solution)/shard_map/all_to_all | solution.py:63
  91.9 1.3 broadcast_select_fusion.5
  93.2 7.7 %collective-permute-start.10 = (bf16[7,96,128]{2,1,0:T(8,128)(2,1)}, bf16[7,96,128]{2,1,0:T(8,128)(2,1)}, u32[]{:S(2)}, u32[]{:S(2)}) collective-permute-start(bf16[7,96,128]{2,1,0:T(8,128)(2,1)} %broadcast_select_fusion.5), channel_id=1, source_target_pairs={{0,64},{4,68},{8,72},{12,76},{16,80},{20,84},{24,88},{28,92},{32,9... | collective-permute-start | bytes 516104 | tf_op jit(solution)/shard_map/ppermute | solution.py:12
  104.2 79.7 %collective-permute-done.10 = bf16[7,96,128]{2,1,0:T(8,128)(2,1)} collective-permute-done((bf16[7,96,128]{2,1,0:T(8,128)(2,1)}, bf16[7,96,128]{2,1,0:T(8,128)(2,1)}, u32[]{:S(2)}, u32[]{:S(2)}) %collective-permute-start.10) | collective-permute-done | bytes 172064 | tf_op jit(solution)/shard_map/ppermute | solution.py:12
  183.9 8.0 %collective-permute-start.11 = (bf16[7,96,128]{2,1,0:T(8,128)(2,1)}, bf16[7,96,128]{2,1,0:T(8,128)(2,1)S(1)}, u32[]{:S(2)}, u32[]{:S(2)}) collective-permute-start(bf16[7,96,128]{2,1,0:T(8,128)(2,1)} %broadcast_select_fusion.3), channel_id=1, source_target_pairs={{0,448},{4,452},{8,456},{12,460},{16,464},{20,468},{24,472},{28,47... | collective-permute-start | bytes 516104 | tf_op jit(solution)/shard_map/ppermute | solution.py:12
  192.0 1.9 stack.18
  193.9 4.8 %all-to-all-start.2 = ((bf16[4,7,96,128]{3,2,1,0:T(8,128)(2,1)}), bf16[4,7,96,128]{3,2,1,0:T(8,128)(2,1)}, u32[]{:S(2)}, u32[]{:S(2)}) async-start(bf16[4,7,96,128]{3,2,1,0:T(8,128)(2,1)} %stack.18), calls=%async_computation.2 | async-start | bytes 1376256 | tf_op jit(solution)/shard_map/all_to_all | solution.py:63
  198.7 21.4 %all_gather.6 = bf16[8,384,128]{2,1,0:T(8,128)(2,1)} all-gather(bf16[8,96,128]{2,1,0:T(8,128)(2,1)S(1)} %copy-done.3), channel_id=1, replica_groups=mesh['dom'=128,'field'=4] {'field'}, dimensions={1}, use_global_device_ids=true | all-gather | bytes 983040 | tf_op jit(solution)/shard_map/all_gather | solution.py:55
  221.3 2.7 gather_fusion
  224.0 1.9 collective-permute-start
  226.9 4.5 %all-to-all-start.3 = ((bf16[4,7,96,128]{3,2,1,0:T(8,128)(2,1)}), bf16[4,7,96,128]{3,2,1,0:T(8,128)(2,1)}, u32[]{:S(2)}, u32[]{:S(2)}) async-start(bf16[4,7,96,128]{3,2,1,0:T(8,128)(2,1)} %stack.19), calls=%async_computation.3 | async-start | bytes 1376256 | tf_op jit(solution)/shard_map/all_to_all | solution.py:63
  231.4 2.2 select_dynamic-update-slice_fusion.1
  233.6 5.7 %collective-permute-start.1 = (s32[7]{0:T(128)S(1)}, s32[7]{0:T(128)S(1)}, u32[]{:S(2)}, u32[]{:S(2)}) collective-permute-start(s32[7]{0:T(128)S(1)} %copy-done.20), channel_id=1, source_target_pairs={{0,508},{4,0},{8,4},{12,8},{16,12},{20,16},{24,20},{28,24},{32,28}... | collective-permute-start | bytes 92 | tf_op jit(solution)/shard_map/ppermute | solution.py:12
  240.6 3.2 collective-permute-start.2
  243.9 11.8 %collective-permute-done.2 = s32[7]{0:T(128)S(1)} collective-permute-done((s32[7]{0:T(128)S(1)}, s32[7]{0:T(128)S(1)}, u32[]{:S(2)}, u32[]{:S(2)}) %collective-permute-start.2) | collective-permute-done | bytes 60 | tf_op jit(solution)/shard_map/ppermute | solution.py:12
  255.7 4.0 collective-permute-start.3
  259.7 10.1 %collective-permute-done.3 = s32[7]{0:T(128)S(1)} collective-permute-done((s32[7]{0:T(128)S(1)}, s32[7]{0:T(128)S(1)}, u32[]{:S(2)}, u32[]{:S(2)}) %collective-permute-start.3) | collective-permute-done | bytes 60 | tf_op jit(solution)/shard_map/ppermute | solution.py:12
  275.1 2.1 copy.13
  277.2 2.0 copy.14
  279.2 2.0 copy.15
  282.5 2.0 constant_dynamic-update-slice_fusion.7
  287.2 2.9 fusion.19
  290.1 1.7 fusion.2
  292.8 1.6 gather_fusion.6
  295.1 1.9 collective-permute-start.12
  297.0 6.9 %collective-permute-done.12 = bf16[7,96,128]{2,1,0:T(8,128)(2,1)S(1)} collective-permute-done((bf16[7,96,128]{2,1,0:T(8,128)(2,1)S(1)}, bf16[7,96,128]{2,1,0:T(8,128)(2,1)S(1)}, u32[]{:S(2)}, u32[]{:S(2)}) %collective-permute-start.12) | collective-permute-done | bytes 172064 | tf_op jit(solution)/shard_map/ppermute | solution.py:12
  304.9 4.5 %all-to-all-start.4 = ((bf16[4,7,96,128]{3,2,1,0:T(8,128)(2,1)}), bf16[4,7,96,128]{3,2,1,0:T(8,128)(2,1)}, u32[]{:S(2)}, u32[]{:S(2)}) async-start(bf16[4,7,96,128]{3,2,1,0:T(8,128)(2,1)} %stack.20), calls=%async_computation.4 | async-start | bytes 1376256 | tf_op jit(solution)/shard_map/all_to_all | solution.py:63
  310.1 1.9 collective-permute-start.13
  312.0 2.9 collective-permute-done.13
  314.9 3.5 all-to-all-done.4
  319.4 4.2 all-to-all-start.5
  324.9 4.2 collective-permute-start.14
  329.0 16.1 %collective-permute-done.14 = bf16[7,96,128]{2,1,0:T(8,128)(2,1)S(1)} collective-permute-done((bf16[7,96,128]{2,1,0:T(8,128)(2,1)S(1)}, bf16[7,96,128]{2,1,0:T(8,128)(2,1)S(1)}, u32[]{:S(2)}, u32[]{:S(2)}) %collective-permute-start.14) | collective-permute-done | bytes 172064 | tf_op jit(solution)/shard_map/ppermute | solution.py:12
  346.1 4.5 %all-to-all-start.6 = ((bf16[4,7,96,128]{3,2,1,0:T(8,128)(2,1)}), bf16[4,7,96,128]{3,2,1,0:T(8,128)(2,1)}, u32[]{:S(2)}, u32[]{:S(2)}) async-start(bf16[4,7,96,128]{3,2,1,0:T(8,128)(2,1)} %stack.22), calls=%async_computation.6 | async-start | bytes 1376256 | tf_op jit(solution)/shard_map/all_to_all | solution.py:63
  351.6 5.8 %collective-permute-start.15 = (bf16[7,96,128]{2,1,0:T(8,128)(2,1)S(1)}, bf16[7,96,128]{2,1,0:T(8,128)(2,1)S(1)}, u32[]{:S(2)}, u32[]{:S(2)}) collective-permute-start(bf16[7,96,128]{2,1,0:T(8,128)(2,1)S(1)} %broadcast_select_fusion.2), channel_id=1, source_target_pairs={{0,448},{4,452},{8,456},{12,460},{16,464},{20,468},{24,472},{28,47... | collective-permute-start | bytes 516104 | tf_op jit(solution)/shard_map/ppermute | solution.py:12
  357.4 12.7 %collective-permute-done.15 = bf16[7,96,128]{2,1,0:T(8,128)(2,1)S(1)} collective-permute-done((bf16[7,96,128]{2,1,0:T(8,128)(2,1)S(1)}, bf16[7,96,128]{2,1,0:T(8,128)(2,1)S(1)}, u32[]{:S(2)}, u32[]{:S(2)}) %collective-permute-start.15) | collective-permute-done | bytes 172064 | tf_op jit(solution)/shard_map/ppermute | solution.py:12
  371.1 4.5 %all-to-all-start.7 = ((bf16[4,7,96,128]{3,2,1,0:T(8,128)(2,1)}), bf16[4,7,96,128]{3,2,1,0:T(8,128)(2,1)}, u32[]{:S(2)}, u32[]{:S(2)}) async-start(bf16[4,7,96,128]{3,2,1,0:T(8,128)(2,1)} %stack.23), calls=%async_computation.7 | async-start | bytes 1376256 | tf_op jit(solution)/shard_map/all_to_all | solution.py:63
  375.6 21.7 %all_gather.7 = bf16[8,384,128]{2,1,0:T(8,128)(2,1)} all-gather(bf16[8,96,128]{2,1,0:T(8,128)(2,1)S(1)} %copy-done.4), channel_id=1, replica_groups=mesh['dom'=128,'field'=4] {'field'}, dimensions={1}, use_global_device_ids=true | all-gather | bytes 983040 | tf_op jit(solution)/shard_map/all_gather | solution.py:55
  397.3 2.7 gather_fusion.5
  400.0 2.2 select_dynamic-update-slice_fusion
  402.2 2.1 copy.18
  404.3 2.0 copy.19
  406.3 2.0 copy.20
  409.6 2.0 constant_dynamic-update-slice_fusion.11
  414.3 2.9 fusion.20
  417.2 1.7 fusion
  (105 shorter events, 32.3 us)
Async XLA Ops:
  0.6 291.1 %copy-start = (bf16[8,96,384]{2,1,0:T(8,128)(2,1)S(1)}, bf16[8,96,384]{2,1,0:T(8,128)(2,1)}, u32[]{:S(2)}) copy-start(bf16[8,96,384]{2,1,0:T(8,128)(2,1)} %param.13) | copy-start | bytes 1769476
  2.1 21.3 %copy-start.14 = (pred[7]{0:T(512)(128)(4,1)}, pred[7]{0:T(512)(128)(4,1)S(1)}, u32[]{:S(2)}) copy-start(pred[7]{0:T(512)(128)(4,1)S(1)} %get-tuple-element.24) | copy-start | bytes 25
  2.1 21.3 %copy-start.16 = (pred[7]{0:T(512)(128)(4,1)}, pred[7]{0:T(512)(128)(4,1)S(1)}, u32[]{:S(2)}) copy-start(pred[7]{0:T(512)(128)(4,1)S(1)} %get-tuple-element.26) | copy-start | bytes 25
  3.7 50.5 %collective-permute-start.8 = (bf16[7,96,128]{2,1,0:T(8,128)(2,1)S(1)}, bf16[7,96,128]{2,1,0:T(8,128)(2,1)S(1)}, u32[]{:S(2)}, u32[]{:S(2)}) collective-permute-start(bf16[7,96,128]{2,1,0:T(8,128)(2,1)S(1)} %broadcast_select_fusion.9), channel_id=1, source_target_pairs={{0,4},{4,8},{8,12},{12,16},{16,20},{20,24},{24,28},{28,32},{32,36}... | collective-permute-start | bytes 516104 | tf_op jit(solution)/shard_map/ppermute | solution.py:12
  7.9 15.5 %copy-start.21 = (s32[35]{0:T(128)S(1)}, s32[35]{0:T(128)}, u32[]{:S(2)}) copy-start(s32[35]{0:T(128)} %param.16) | copy-start | bytes 424
  7.9 77.1 %collective-permute-start.9 = (bf16[7,96,128]{2,1,0:T(8,128)(2,1)}, bf16[7,96,128]{2,1,0:T(8,128)(2,1)}, u32[]{:S(2)}, u32[]{:S(2)}) collective-permute-start(bf16[7,96,128]{2,1,0:T(8,128)(2,1)} %broadcast_select_fusion.7), channel_id=1, source_target_pairs={{0,508},{4,0},{8,4},{12,8},{16,12},{20,16},{24,20},{28,24},{32,28}... | collective-permute-start | bytes 516104 | tf_op jit(solution)/shard_map/ppermute | solution.py:12
  50.0 4.1 copy-start.22
  55.2 29.8 %all-to-all-start = ((bf16[4,7,96,128]{3,2,1,0:T(8,128)(2,1)}), bf16[4,7,96,128]{3,2,1,0:T(8,128)(2,1)}, u32[]{:S(2)}, u32[]{:S(2)}) async-start(bf16[4,7,96,128]{3,2,1,0:T(8,128)(2,1)} %stack.16), calls=%async_computation | async-start | bytes 1376256 | tf_op jit(solution)/shard_map/all_to_all | solution.py:63
  59.8 24.6 %copy-start.3 = (bf16[8,96,128]{2,1,0:T(8,128)(2,1)S(1)}, bf16[8,96,128]{2,1,0:T(8,128)(2,1)}, u32[]{:S(2)}) copy-start(bf16[8,96,128]{2,1,0:T(8,128)(2,1)} %param.11) | copy-start | bytes 589828
  61.3 209.3 %collective-permute-start.4 = (bf16[7,96,384]{2,1,0:T(8,128)(2,1)}, bf16[7,96,384]{2,1,0:T(8,128)(2,1)}, u32[]{:S(2)}, u32[]{:S(2)}) collective-permute-start(bf16[7,96,384]{2,1,0:T(8,128)(2,1)} %get-tuple-element.17), channel_id=1, source_target_pairs={{0,4},{4,8},{8,12},{12,16},{16,20},{20,24},{24,28},{28,32},{32,36}... | collective-permute-start | bytes 1548296 | tf_op jit(solution)/shard_map/ppermute | solution.py:12
  63.2 208.5 %collective-permute-start.5 = (bf16[7,96,384]{2,1,0:T(8,128)(2,1)}, bf16[7,96,384]{2,1,0:T(8,128)(2,1)}, u32[]{:S(2)}, u32[]{:S(2)}) collective-permute-start(bf16[7,96,384]{2,1,0:T(8,128)(2,1)} %get-tuple-element.16), channel_id=1, source_target_pairs={{0,508},{4,0},{8,4},{12,8},{16,12},{20,16},{24,20},{28,24},{32,28}... | collective-permute-start | bytes 1548296 | tf_op jit(solution)/shard_map/ppermute | solution.py:12
  68.9 203.9 %collective-permute-start.6 = (bf16[7,96,384]{2,1,0:T(8,128)(2,1)}, bf16[7,96,384]{2,1,0:T(8,128)(2,1)}, u32[]{:S(2)}, u32[]{:S(2)}) collective-permute-start(bf16[7,96,384]{2,1,0:T(8,128)(2,1)} %get-tuple-element.15), channel_id=1, source_target_pairs={{0,64},{4,68},{8,72},{12,76},{16,80},{20,84},{24,88},{28,92},{32,9... | collective-permute-start | bytes 1548296 | tf_op jit(solution)/shard_map/ppermute | solution.py:12
  77.6 196.4 %collective-permute-start.7 = (bf16[7,96,384]{2,1,0:T(8,128)(2,1)}, bf16[7,96,384]{2,1,0:T(8,128)(2,1)}, u32[]{:S(2)}, u32[]{:S(2)}) collective-permute-start(bf16[7,96,384]{2,1,0:T(8,128)(2,1)} %get-tuple-element.14), channel_id=1, source_target_pairs={{0,448},{4,452},{8,456},{12,460},{16,464},{20,468},{24,472},{28,47... | collective-permute-start | bytes 1548296 | tf_op jit(solution)/shard_map/ppermute | solution.py:12
  86.9 133.2 %copy-start.9 = (s32[35]{0:T(128)S(1)}, s32[35]{0:T(128)}, u32[]{:S(2)}) copy-start(s32[35]{0:T(128)} %param.15) | copy-start | bytes 424
  86.9 105.0 %all-to-all-start.1 = ((bf16[4,7,96,128]{3,2,1,0:T(8,128)(2,1)}), bf16[4,7,96,128]{3,2,1,0:T(8,128)(2,1)}, u32[]{:S(2)}, u32[]{:S(2)}) async-start(bf16[4,7,96,128]{3,2,1,0:T(8,128)(2,1)} %stack.17), calls=%async_computation.1 | async-start | bytes 1376256 | tf_op jit(solution)/shard_map/all_to_all | solution.py:63
  93.2 90.7 %collective-permute-start.10 = (bf16[7,96,128]{2,1,0:T(8,128)(2,1)}, bf16[7,96,128]{2,1,0:T(8,128)(2,1)}, u32[]{:S(2)}, u32[]{:S(2)}) collective-permute-start(bf16[7,96,128]{2,1,0:T(8,128)(2,1)} %broadcast_select_fusion.5), channel_id=1, source_target_pairs={{0,64},{4,68},{8,72},{12,76},{16,80},{20,84},{24,88},{28,92},{32,9... | collective-permute-start | bytes 516104 | tf_op jit(solution)/shard_map/ppermute | solution.py:12
  183.9 40.1 %collective-permute-start.11 = (bf16[7,96,128]{2,1,0:T(8,128)(2,1)}, bf16[7,96,128]{2,1,0:T(8,128)(2,1)S(1)}, u32[]{:S(2)}, u32[]{:S(2)}) collective-permute-start(bf16[7,96,128]{2,1,0:T(8,128)(2,1)} %broadcast_select_fusion.3), channel_id=1, source_target_pairs={{0,448},{4,452},{8,456},{12,460},{16,464},{20,468},{24,472},{28,47... | collective-permute-start | bytes 516104 | tf_op jit(solution)/shard_map/ppermute | solution.py:12
  193.9 32.0 %all-to-all-start.2 = ((bf16[4,7,96,128]{3,2,1,0:T(8,128)(2,1)}), bf16[4,7,96,128]{3,2,1,0:T(8,128)(2,1)}, u32[]{:S(2)}, u32[]{:S(2)}) async-start(bf16[4,7,96,128]{3,2,1,0:T(8,128)(2,1)} %stack.18), calls=%async_computation.2 | async-start | bytes 1376256 | tf_op jit(solution)/shard_map/all_to_all | solution.py:63
  224.0 9.6 %collective-permute-start = (s32[7]{0:T(128)}, s32[7]{0:T(128)}, u32[]{:S(2)}, u32[]{:S(2)}) collective-permute-start(s32[7]{0:T(128)} %get-tuple-element.21), channel_id=1, source_target_pairs={{0,4},{4,8},{8,12},{12,16},{16,20},{20,24},{24,28},{28,32},{32,36}... | collective-permute-start | bytes 92 | tf_op jit(solution)/shard_map/ppermute | solution.py:12
  226.9 6.7 %copy-start.20 = (s32[7]{0:T(128)S(1)}, s32[7]{0:T(128)}, u32[]{:S(2)}) copy-start(s32[7]{0:T(128)} %get-tuple-element.20) | copy-start | bytes 88
  226.9 13.7 %copy-start.19 = (s32[7]{0:T(128)S(1)}, s32[7]{0:T(128)}, u32[]{:S(2)}) copy-start(s32[7]{0:T(128)} %get-tuple-element.23) | copy-start | bytes 88
  226.9 28.8 %copy-start.18 = (s32[7]{0:T(128)S(1)}, s32[7]{0:T(128)}, u32[]{:S(2)}) copy-start(s32[7]{0:T(128)} %get-tuple-element.19) | copy-start | bytes 88
  226.9 43.0 %copy-start.17 = (s32[7]{0:T(128)S(1)}, s32[7]{0:T(128)}, u32[]{:S(2)}) copy-start(s32[7]{0:T(128)} %get-tuple-element.22) | copy-start | bytes 88
  226.9 54.3 %all-to-all-start.3 = ((bf16[4,7,96,128]{3,2,1,0:T(8,128)(2,1)}), bf16[4,7,96,128]{3,2,1,0:T(8,128)(2,1)}, u32[]{:S(2)}, u32[]{:S(2)}) async-start(bf16[4,7,96,128]{3,2,1,0:T(8,128)(2,1)} %stack.19), calls=%async_computation.3 | async-start | bytes 1376256 | tf_op jit(solution)/shard_map/all_to_all | solution.py:63
  233.6 7.0 %collective-permute-start.1 = (s32[7]{0:T(128)S(1)}, s32[7]{0:T(128)S(1)}, u32[]{:S(2)}, u32[]{:S(2)}) collective-permute-start(s32[7]{0:T(128)S(1)} %copy-done.20), channel_id=1, source_target_pairs={{0,508},{4,0},{8,4},{12,8},{16,12},{20,16},{24,20},{28,24},{32,28}... | collective-permute-start | bytes 92 | tf_op jit(solution)/shard_map/ppermute | solution.py:12
  240.6 15.1 %collective-permute-start.2 = (s32[7]{0:T(128)S(1)}, s32[7]{0:T(128)S(1)}, u32[]{:S(2)}, u32[]{:S(2)}) collective-permute-start(s32[7]{0:T(128)S(1)} %copy-done.19), channel_id=1, source_target_pairs={{0,64},{4,68},{8,72},{12,76},{16,80},{20,84},{24,88},{28,92},{32,9... | collective-permute-start | bytes 92 | tf_op jit(solution)/shard_map/ppermute | solution.py:12
  255.7 14.2 %collective-permute-start.3 = (s32[7]{0:T(128)S(1)}, s32[7]{0:T(128)S(1)}, u32[]{:S(2)}, u32[]{:S(2)}) collective-permute-start(s32[7]{0:T(128)S(1)} %copy-done.18), channel_id=1, source_target_pairs={{0,448},{4,452},{8,456},{12,460},{16,464},{20,468},{24,472},{28,47... | collective-permute-start | bytes 92 | tf_op jit(solution)/shard_map/ppermute | solution.py:12
  270.6 19.5 %copy-start.11 = (s32[35]{0:T(128)}, s32[35]{0:T(128)S(1)}, u32[]{:S(2)}) copy-start(s32[35]{0:T(128)S(1)} %concatenate.12) | copy-start | bytes 424
  281.2 3.3 copy-start.7
  281.2 4.2 copy-start.5
  290.1 1.7 copy-start.1
  292.8 16.6 %copy-start.4 = (bf16[8,96,128]{2,1,0:T(8,128)(2,1)S(1)}, bf16[8,96,128]{2,1,0:T(8,128)(2,1)}, u32[]{:S(2)}) copy-start(bf16[8,96,128]{2,1,0:T(8,128)(2,1)} %fusion.7) | copy-start | bytes 589828
  294.4 15.6 %copy-start.15 = (pred[7]{0:T(512)(128)(4,1)S(1)}, pred[7]{0:T(512)(128)(4,1)}, u32[]{:S(2)}) copy-start(pred[7]{0:T(512)(128)(4,1)} %copy-done.14) | copy-start | bytes 25
  295.1 8.8 %collective-permute-start.12 = (bf16[7,96,128]{2,1,0:T(8,128)(2,1)S(1)}, bf16[7,96,128]{2,1,0:T(8,128)(2,1)S(1)}, u32[]{:S(2)}, u32[]{:S(2)}) collective-permute-start(bf16[7,96,128]{2,1,0:T(8,128)(2,1)S(1)} %broadcast_select_fusion.8), channel_id=1, source_target_pairs={{0,4},{4,8},{8,12},{12,16},{16,20},{20,24},{24,28},{28,32},{32,36}... | collective-permute-start | bytes 516104 | tf_op jit(solution)/shard_map/ppermute | solution.py:12
  304.9 13.5 %all-to-all-start.4 = ((bf16[4,7,96,128]{3,2,1,0:T(8,128)(2,1)}), bf16[4,7,96,128]{3,2,1,0:T(8,128)(2,1)}, u32[]{:S(2)}, u32[]{:S(2)}) async-start(bf16[4,7,96,128]{3,2,1,0:T(8,128)(2,1)} %stack.20), calls=%async_computation.4 | async-start | bytes 1376256 | tf_op jit(solution)/shard_map/all_to_all | solution.py:63
  310.0 41.4 %copy-start.13 = (pred[7]{0:T(512)(128)(4,1)S(1)}, pred[7]{0:T(512)(128)(4,1)}, u32[]{:S(2)}) copy-start(pred[7]{0:T(512)(128)(4,1)} %get-tuple-element.4) | copy-start | bytes 25
  310.1 4.8 %collective-permute-start.13 = (bf16[7,96,128]{2,1,0:T(8,128)(2,1)S(1)}, bf16[7,96,128]{2,1,0:T(8,128)(2,1)S(1)}, u32[]{:S(2)}, u32[]{:S(2)}) collective-permute-start(bf16[7,96,128]{2,1,0:T(8,128)(2,1)S(1)} %broadcast_select_fusion.6), channel_id=1, source_target_pairs={{0,508},{4,0},{8,4},{12,8},{16,12},{20,16},{24,20},{28,24},{32,28}... | collective-permute-start | bytes 516104 | tf_op jit(solution)/shard_map/ppermute | solution.py:12
  319.4 25.8 %all-to-all-start.5 = ((bf16[4,7,96,128]{3,2,1,0:T(8,128)(2,1)}), bf16[4,7,96,128]{3,2,1,0:T(8,128)(2,1)}, u32[]{:S(2)}, u32[]{:S(2)}) async-start(bf16[4,7,96,128]{3,2,1,0:T(8,128)(2,1)} %stack.21), calls=%async_computation.5 | async-start | bytes 1376256 | tf_op jit(solution)/shard_map/all_to_all | solution.py:63
  324.9 20.3 %collective-permute-start.14 = (bf16[7,96,128]{2,1,0:T(8,128)(2,1)S(1)}, bf16[7,96,128]{2,1,0:T(8,128)(2,1)S(1)}, u32[]{:S(2)}, u32[]{:S(2)}) collective-permute-start(bf16[7,96,128]{2,1,0:T(8,128)(2,1)S(1)} %broadcast_select_fusion.4), channel_id=1, source_target_pairs={{0,64},{4,68},{8,72},{12,76},{16,80},{20,84},{24,88},{28,92},{32,9... | collective-permute-start | bytes 516104 | tf_op jit(solution)/shard_map/ppermute | solution.py:12
  346.1 24.0 %all-to-all-start.6 = ((bf16[4,7,96,128]{3,2,1,0:T(8,128)(2,1)}), bf16[4,7,96,128]{3,2,1,0:T(8,128)(2,1)}, u32[]{:S(2)}, u32[]{:S(2)}) async-start(bf16[4,7,96,128]{3,2,1,0:T(8,128)(2,1)} %stack.22), calls=%async_computation.6 | async-start | bytes 1376256 | tf_op jit(solution)/shard_map/all_to_all | solution.py:63
  350.6 49.4 %copy-start.10 = (pred[7]{0:T(512)(128)(4,1)S(1)}, pred[7]{0:T(512)(128)(4,1)}, u32[]{:S(2)}) copy-start(pred[7]{0:T(512)(128)(4,1)} %get-tuple-element.28) | copy-start | bytes 25
  351.6 18.5 %collective-permute-start.15 = (bf16[7,96,128]{2,1,0:T(8,128)(2,1)S(1)}, bf16[7,96,128]{2,1,0:T(8,128)(2,1)S(1)}, u32[]{:S(2)}, u32[]{:S(2)}) collective-permute-start(bf16[7,96,128]{2,1,0:T(8,128)(2,1)S(1)} %broadcast_select_fusion.2), channel_id=1, source_target_pairs={{0,448},{4,452},{8,456},{12,460},{16,464},{20,468},{24,472},{28,47... | collective-permute-start | bytes 516104 | tf_op jit(solution)/shard_map/ppermute | solution.py:12
  371.1 37.2 %all-to-all-start.7 = ((bf16[4,7,96,128]{3,2,1,0:T(8,128)(2,1)}), bf16[4,7,96,128]{3,2,1,0:T(8,128)(2,1)}, u32[]{:S(2)}, u32[]{:S(2)}) async-start(bf16[4,7,96,128]{3,2,1,0:T(8,128)(2,1)} %stack.23), calls=%async_computation.7 | async-start | bytes 1376256 | tf_op jit(solution)/shard_map/all_to_all | solution.py:63
  408.3 3.3 copy-start.8
  408.3 4.2 copy-start.6
  414.3 2.9 copy-start.12
  417.2 1.7 copy-start.2
